TPU v7x, 768 devices: a whole 4x8x12 slice. The times are simulated.
768 devices in a mesh: ctx: 48 (over z, x), seq: 16 (over y, core).
Axes of the slice: x: 4, y: 8, z: 12, core: 2. Of those that a mesh axis runs over, the one named last changes fastest.
Arguments:
- queries: bfloat16 [24576, 8192], P('ctx', 'seq'), may hold values from -0.375 to 0.375
- keys: bfloat16 [24576, 8192], P('ctx', 'seq'), may hold values from -0.375 to 0.375
- values: bfloat16 [24576, 8192], P('ctx', 'seq'), may hold values from -6 to 6
- out_grad: bfloat16 [24576, 8192], P('ctx', 'seq'), may hold values from -0.375 to 0.375
Outputs:
- attended: bfloat16 [24576, 8192], P('ctx', 'seq')
- query_grad: bfloat16 [24576, 8192], P('ctx', 'seq')
- key_grad: bfloat16 [24576, 8192], P('ctx', 'seq')
- value_grad: bfloat16 [24576, 8192], P('ctx', 'seq')
All inputs are finite; a program needn't handle non-finite values.
Results may differ from a plain program's by a relative error of at most 0.0049.
Values sent between devices are 32-bit elements; how exact they have to be, the bound alone decides.
A program may use at most 128 MiB of HBM per device.

v0:
```python
import jax
import jax.numpy as jnp
from jax import lax
from jax.sharding import PartitionSpec as P

DH = 128
BLOCK = 128


def prefix(part, axis, combine, identity, reverse):
    count = lax.axis_size(axis)
    place = lax.axis_index(axis)
    ahead = count - 1 - place if reverse else place
    gathered = lax.all_gather(part, axis)
    state = jnp.zeros_like(part) + jnp.asarray(identity, part.dtype)

    def one(turn, state):
        source = count - 1 - turn if reverse else turn
        return combine(state, lax.dynamic_index_in_dim(gathered, source, 0, False))

    return lax.fori_loop(0, ahead, one, state)


def add_states(earlier, later):
    return earlier + later


def body(queries, keys, values, out_grad):
    count = queries.shape[0]
    heads = queries.shape[1] // DH
    nblocks = count // BLOCK
    shape = (nblocks, BLOCK, heads, DH)
    qloc = queries.reshape(shape)
    kloc = keys.reshape(shape)
    vloc = values.reshape(shape)
    gloc = out_grad.reshape(shape)
    f32 = jnp.float32
    kv_blocks = jnp.einsum("bthi,bthj->bhij", kloc, vloc, preferred_element_type=f32)
    qg_blocks = jnp.einsum("bthi,bthj->bhij", qloc, gloc, preferred_element_type=f32)
    kv_run = jnp.sum(kv_blocks, axis=0)
    qg_run = jnp.sum(qg_blocks, axis=0)
    kv_before = prefix(kv_run, "ctx", add_states, jnp.zeros_like(kv_run), False)
    qg_after = prefix(qg_run, "ctx", add_states, jnp.zeros_like(qg_run), True)
    kv_local = lax.cumsum(kv_blocks, axis=0) - kv_blocks
    qg_local = lax.cumsum(qg_blocks, axis=0, reverse=True) - qg_blocks
    prefix_low = (kv_before[None] + kv_local).astype(jnp.bfloat16)
    suffix_low = (qg_after[None] + qg_local).astype(jnp.bfloat16)
    rows = lax.broadcasted_iota(jnp.int32, (BLOCK, BLOCK), 0)
    cols = lax.broadcasted_iota(jnp.int32, (BLOCK, BLOCK), 1)
    causal = (cols <= rows)[None, None]
    attn = jnp.where(
        causal, jnp.einsum("bthi,bshi->bhts", qloc, kloc, preferred_element_type=f32), 0.0
    ).astype(jnp.bfloat16)
    grads = jnp.where(
        causal, jnp.einsum("bthj,bshj->bhts", gloc, vloc, preferred_element_type=f32), 0.0
    ).astype(jnp.bfloat16)
    attended = jnp.einsum("bhts,bshj->bthj", attn, vloc, preferred_element_type=f32)
    attended = attended + jnp.einsum(
        "bthi,bhij->bthj", qloc, prefix_low, preferred_element_type=f32
    )
    query_grad = jnp.einsum("bhts,bshi->bthi", grads, kloc, preferred_element_type=f32)
    query_grad = query_grad + jnp.einsum(
        "bthj,bhij->bthi", gloc, prefix_low, preferred_element_type=f32
    )
    key_grad = jnp.einsum("bhts,bthi->bshi", grads, qloc, preferred_element_type=f32)
    key_grad = key_grad + jnp.einsum(
        "bshj,bhij->bshi", vloc, suffix_low, preferred_element_type=f32
    )
    value_grad = jnp.einsum("bhts,bthj->bshj", attn, gloc, preferred_element_type=f32)
    value_grad = value_grad + jnp.einsum(
        "bshi,bhij->bshj", kloc, suffix_low, preferred_element_type=f32
    )
    flat = (count, heads * DH)
    return (
        attended.astype(jnp.bfloat16).reshape(flat),
        query_grad.astype(jnp.bfloat16).reshape(flat),
        key_grad.astype(jnp.bfloat16).reshape(flat),
        value_grad.astype(jnp.bfloat16).reshape(flat),
    )


def solution(mesh):
    in_specs = (P("ctx", "seq"), P("ctx", "seq"), P("ctx", "seq"), P("ctx", "seq"))
    out_specs = (P("ctx", "seq"), P("ctx", "seq"), P("ctx", "seq"), P("ctx", "seq"))
    return jax.shard_map(body, mesh=mesh, in_specs=in_specs, out_specs=out_specs, check_vma=False)
```

profile of v0, /device:TPU:1, one launch (start us, length us, event | category | flops | bytes accessed | tf_op | source)
XLA Modules:
  0.0 389.0 jit_solution(8888269578552016128)
XLA Ops:
  7.2 1.2 reshape.43
  8.4 1.2 reshape.42
  9.6 1.1 fusion.28
  10.7 2.0 reshape.45
  12.6 1.2 reshape.41
  13.8 1.0 copy.77
  14.8 2.2 fusion.29
  17.1 1.5 fusion.9
  18.7 1.6 fusion.8
  20.2 1.3 convolution_bitcast_fusion.7
  21.5 2.5 convolution_bitcast_fusion.2
  24.0 1.3 convolution_bitcast_fusion.6
  25.2 2.5 convolution_bitcast_fusion.4
  27.8 144.3 %all-gather.5.cloned.1.call-done = f32[192,128,128]{2,1,0:T(8,128)} async-done(((f32[4,128,128]{2,1,0:T(8,128)}), f32[192,128,128]{2,1,0:T(8,128)}) %all-gather.5.cloned.1.call-update) | async-done | bytes 12582928 | tf_op jit(solution)/shard_map/all_gather | solution.py:14
  172.3 1.9 fusion.10
  174.2 1.2 copy.74
  175.4 1.7 fusion.12
  177.1 1.2 copy.68
  178.3 147.5 %all-gather.7.cloned.1.call-done = f32[192,128,128]{2,1,0:T(8,128)} async-done(((f32[4,128,128]{2,1,0:T(8,128)}), f32[192,128,128]{2,1,0:T(8,128)}) %all-gather.7.cloned.1.call-update) | async-done | bytes 12582928 | tf_op jit(solution)/shard_map/all_gather | solution.py:14
  325.9 48.6 %while.23 = (s32[]{:T(128)}, f32[4,128,128]{2,1,0:T(8,128)S(1)}, s32[]{:T(128)}, f32[48,4,128,128]{3,2,1,0:T(8,128)}, s32[]{:T(128)}, /*index=5*/s32[]{:T(128)}, s32[]{:T(128)}, s32[]{:T(128)}) while((s32[]{:T(128)}, f32[4,128,128]{2,1,0:T(8,128)S(1)}, s32[]{:T(128)}, f32[48,4,128,128]{3,2,1,0:T(8,128)}, s32[]{:T(128)}, /*index=5*/s32[]{:T(128)}, ...), condition=%wide.region_6.7_spmd, body=%wide.region_5.6_spmd.sunk | while | flops 65542 | bytes 786575 | solution.py:21
  325.9 1.0 bitcast_add_fusion.5
  327.0 1.0 bitcast_add_fusion.5
  328.0 1.0 bitcast_add_fusion.5
  335.2 1.0 bitcast_add_fusion.5
  336.3 1.0 bitcast_add_fusion.5
  337.3 1.0 bitcast_add_fusion.5
  345.6 1.0 bitcast_add_fusion.5
  346.6 1.0 bitcast_add_fusion.5
  374.7 1.5 fusion.13
  376.6 1.7 fusion.11
  378.8 2.3 copy_bitcast_fusion.2
  381.1 1.1 copy_bitcast_fusion
  (51 shorter events, 40.8 us)
Async XLA Ops:
  7.2 164.9 %all-gather.5.cloned.1.call-start = ((), (), s32[]{:S(2)}) async-start(), calls=%async_computation | async-start | bytes 12845056 | tf_op jit(solution)/shard_map/all_gather | solution.py:14
  10.6 315.3 %all-gather.7.cloned.1.call-start = ((), (), s32[]{:S(2)}) async-start(), calls=%async_computation.1 | async-start | bytes 12845056 | tf_op jit(solution)/shard_map/all_gather | solution.py:14
Sparse Core Ops, SparseCore 0:
  12.1 159.9 all-gather.4
  176.2 149.5 all-gather.6
where the time goes:
time: 391 us; the launch traced here: 389 us
  waiting for transfers between devices  292 us (75%)
  other arithmetic  47.9 us (12%)
  matrix products  20.8 us (5%)
  between operations  14.2 us (4%)
  local copies, waits for them, and re-layouts  13.2 us (3%)
    all_gather x2, waiting for transfers between devices, prefix(): gathered = lax.all_gather(part, axis)  292 us
    add x47, other arithmetic, add_states(): return earlier + later  47.5 us
  transfers between devices with their start and end apart: 2, of which 2 were waited for; matrix products, arithmetic and copies ran while one was open for 6% of the time, Pallas kernels for 0%

commit v1 on v0

v1 whole, which is shorter than its diff:
```python
import functools

import jax
import jax.numpy as jnp
from jax import lax
from jax.experimental import pallas as pl
from jax.experimental.pallas import tpu as pltpu
from jax.sharding import PartitionSpec as P

DH = 128
BLOCK = 128
X = 4
MESH = pl.DeviceIdType.MESH
F32 = jnp.float32
BF16 = jnp.bfloat16


def dot(a, b, ca, cb):
    return lax.dot_general(a, b, (((ca,), (cb,)), ((), ())), preferred_element_type=F32)


def kernel(
    nz, nb, q_hbm, k_hbm, v_hbm, g_hbm, *refs,
):
    outs = refs[:4]
    (qs, ks, vs, gs, cum, part, xsend, xrecv, tbuf, zrecv, zsend, zpre, xback, before, obuf,
     in_sem, out_sem, xu_s, xu_r, zu_s, zu_r, zd_s, zd_r, xd_s, xd_r) = refs[4:]
    rows = tbuf.shape[1] // nz
    c = lax.axis_index("ctx")
    seq = lax.axis_index("seq")
    z = c // X
    x = c % X

    def xdev(d):
        return (z * X + (x + d) % X, seq)

    def zdev(d):
        return (((z + d) % nz) * X + x, seq)

    zorder = sorted(range(1, nz), key=lambda d: -min(d, nz - d))

    barrier = pltpu.get_barrier_semaphore()
    for d in range(1, X):
        pl.semaphore_signal(barrier, inc=1, device_id=xdev(d), device_id_type=MESH)
    for d in range(1, nz):
        pl.semaphore_signal(barrier, inc=1, device_id=zdev(d), device_id_type=MESH)

    def cols(s):
        return pl.ds(pl.multiple_of(((x + s) % X) * DH, DH), DH)

    slots = (2, 1, 3, 0)
    loads = {}
    for pair in (((k_hbm, ks, 1), (v_hbm, vs, 2)), ((q_hbm, qs, 0), (g_hbm, gs, 3))):
        for s in slots:
            for hbm, buf, i in pair:
                cp = pltpu.make_async_copy(hbm.at[:, cols(s)], buf.at[s], in_sem.at[i, s])
                cp.start()
                loads[i, s] = cp

    for kind in range(2):
        if tbuf.shape[1] > DH:
            lo = DH if kind == 0 else 0
            tbuf[kind, lo:lo + tbuf.shape[1] - DH, :] = jnp.zeros((tbuf.shape[1] - DH, DH), F32)
    base = (0, tbuf.shape[1] - DH)

    def local_state(kind, s):
        a, b = ((ks, vs), (qs, gs))[kind]
        run = jnp.zeros((DH, DH), F32)
        order = range(nb) if kind == 0 else range(nb - 1, -1, -1)
        for blk in order:
            cum[kind, s, blk] = run
            r = pl.ds(blk * BLOCK, BLOCK)
            run = run + dot(a[s, r, :], b[s, r, :], 0, 0)
        return run

    xup = {}
    for kind in range(2):
        for s in slots:
            for i in ((1, 2), (0, 3))[kind]:
                loads[i, s].wait()
            total = local_state(kind, s)
            if s == 0:
                xrecv[kind, x] = total
            else:
                xsend[kind, s] = total
                if kind == 0 and s == slots[0]:
                    pl.semaphore_wait(barrier, X - 1 + nz - 1)
                cp = pltpu.make_async_remote_copy(
                    xsend.at[kind, s], xrecv.at[kind, x], xu_s.at[kind, s], xu_r.at[kind, s],
                    device_id=xdev(s), device_id_type=MESH)
                cp.start()
                xup[kind, s] = cp

    tri = (lax.broadcasted_iota(jnp.int32, (BLOCK, BLOCK), 1)
           <= lax.broadcasted_iota(jnp.int32, (BLOCK, BLOCK), 0))

    def intra(s):
        def one(blk, carry):
            r = pl.ds(pl.multiple_of(blk * BLOCK, BLOCK), BLOCK)
            q, k, v, g = qs[s, r, :], ks[s, r, :], vs[s, r, :], gs[s, r, :]
            attn = jnp.where(tri, dot(q, k, 1, 1), 0.0).astype(BF16)
            grads = jnp.where(tri, dot(g, v, 1, 1), 0.0).astype(BF16)
            part[0, s, r, :] = dot(attn, v, 1, 0)
            part[1, s, r, :] = dot(grads, k, 1, 0)
            part[2, s, r, :] = dot(grads, q, 0, 0)
            part[3, s, r, :] = dot(attn, g, 0, 0)
            return carry

        lax.fori_loop(0, nb, one, 0)

    def wait_xup(kind):
        for d in (1, 3, 2):
            pltpu.make_async_remote_copy(
                xsend.at[kind, d], xrecv.at[kind, (x + X - d) % X], xu_s.at[kind, d], xu_r.at[kind, d],
                device_id=xdev(d), device_id_type=MESH).wait_recv()

    zup, zdn, xdn = {}, {}, {}
    intra(0)
    for kind in range(2):
        wait_xup(kind)
        total = xrecv[kind, 0]
        for i in range(1, X):
            total = total + xrecv[kind, i]
        tbuf[kind, base[kind]:base[kind] + DH, :] = total
        for d in zorder:
            cp = pltpu.make_async_remote_copy(
                tbuf.at[kind, pl.ds(pl.multiple_of(((z + d) % nz) * rows, 8), rows)],
                zrecv.at[kind, z], zu_s.at[kind, d], zu_r.at[kind, d],
                device_id=zdev(d), device_id_type=MESH)
            cp.start()
            zup[kind, d] = cp
        zrecv[kind, z] = tbuf[kind, pl.ds(pl.multiple_of(z * rows, 8), rows), :]

    intra(1)
    for kind in range(2):
        for d in range(1, nz):
            pltpu.make_async_remote_copy(
                tbuf.at[kind, pl.ds(0, rows)], zrecv.at[kind, (z + nz - d) % nz],
                zu_s.at[kind, d], zu_r.at[kind, d],
                device_id=zdev(d), device_id_type=MESH).wait_recv()
        run = jnp.zeros((rows, DH), F32)
        for i in (range(nz) if kind == 0 else range(nz - 1, -1, -1)):
            zsend[kind, i] = run
            run = run + zrecv[kind, i]
        mine = pl.ds(pl.multiple_of(z * rows, 8), rows)
        for d in zorder:
            cp = pltpu.make_async_remote_copy(
                zsend.at[kind, (z + d) % nz], zpre.at[kind, mine], zd_s.at[kind, d], zd_r.at[kind, d],
                device_id=zdev(d), device_id_type=MESH)
            cp.start()
            zdn[kind, d] = cp
        zpre[kind, mine, :] = zsend[kind, z]

    intra(2)
    for kind in range(2):
        for d in range(1, nz):
            pltpu.make_async_remote_copy(
                zsend.at[kind, 0],
                zpre.at[kind, pl.ds(pl.multiple_of(((z + nz - d) % nz) * rows, 8), rows)],
                zd_s.at[kind, d], zd_r.at[kind, d],
                device_id=zdev(d), device_id_type=MESH).wait_recv()
        run = zpre[kind, base[kind]:base[kind] + DH, :]
        for i in (range(X) if kind == 0 else range(X - 1, -1, -1)):
            xback[kind, i] = run
            run = run + xrecv[kind, i]
        for d in (2, 1, 3):
            cp = pltpu.make_async_remote_copy(
                xback.at[kind, (x + d) % X], before.at[kind, X - d], xd_s.at[kind, d], xd_r.at[kind, d],
                device_id=xdev(d), device_id_type=MESH)
            cp.start()
            xdn[kind, d] = cp
        before[kind, 0] = xback[kind, x]

    intra(3)
    stores = []
    for kind in range(2):
        first, second = ((qs, gs), (vs, ks))[kind]
        for s in (0, 1, 3, 2):
            if s:
                d = X - s
                pltpu.make_async_remote_copy(
                    xback.at[kind, d], before.at[kind, s], xd_s.at[kind, d], xd_r.at[kind, d],
                    device_id=xdev(d), device_id_type=MESH).wait_recv()

            def one(blk, carry, kind=kind, s=s):
                r = pl.ds(pl.multiple_of(blk * BLOCK, BLOCK), BLOCK)
                low = (before[kind, s] + cum[kind, s, blk]).astype(BF16)
                if kind == 0:
                    obuf[0, s, r, :] = (part[0, s, r, :] + dot(qs[s, r, :], low, 1, 0)).astype(BF16)
                    obuf[1, s, r, :] = (part[1, s, r, :] + dot(gs[s, r, :], low, 1, 1)).astype(BF16)
                else:
                    obuf[2, s, r, :] = (part[2, s, r, :] + dot(vs[s, r, :], low, 1, 1)).astype(BF16)
                    obuf[3, s, r, :] = (part[3, s, r, :] + dot(ks[s, r, :], low, 1, 0)).astype(BF16)
                return carry

            lax.fori_loop(0, nb, one, 0)
            for o in (2 * kind, 2 * kind + 1):
                cp = pltpu.make_async_copy(obuf.at[o, s], outs[o].at[:, cols(s)], out_sem.at[o, s])
                cp.start()
                stores.append(cp)

    for group in (xup, zup, zdn, xdn):
        for cp in group.values():
            cp.wait_send()
    for cp in stores:
        cp.wait()


def body(nz, queries, keys, values, out_grad):
    count, width = queries.shape
    nb = count // BLOCK
    assert width == X * DH
    rows = -(-(DH // 8) // nz) * 8
    any_spec = pl.BlockSpec(memory_space=pl.ANY)
    vm = pltpu.VMEM
    dma = pltpu.SemaphoreType.DMA
    shape = jax.ShapeDtypeStruct((count, width), BF16)
    return pl.pallas_call(
        functools.partial(kernel, nz, nb),
        out_shape=(shape,) * 4,
        in_specs=[any_spec] * 4,
        out_specs=(any_spec,) * 4,
        scratch_shapes=[
            vm((X, count, DH), BF16),
            vm((X, count, DH), BF16),
            vm((X, count, DH), BF16),
            vm((X, count, DH), BF16),
            vm((2, X, nb, DH, DH), F32),
            vm((4, X, count, DH), F32),
            vm((2, X, DH, DH), F32),
            vm((2, X, DH, DH), F32),
            vm((2, nz * rows, DH), F32),
            vm((2, nz, rows, DH), F32),
            vm((2, nz, rows, DH), F32),
            vm((2, nz * rows, DH), F32),
            vm((2, X, DH, DH), F32),
            vm((2, X, DH, DH), F32),
            vm((4, X, count, DH), BF16),
            dma((4, X)), dma((4, X)),
            dma((2, X)), dma((2, X)),
            dma((2, nz)), dma((2, nz)),
            dma((2, nz)), dma((2, nz)),
            dma((2, X)), dma((2, X)),
        ],
        compiler_params=pltpu.CompilerParams(
            collective_id=0, has_side_effects=True, vmem_limit_bytes=48 * 1024 * 1024),
    )(queries, keys, values, out_grad)


def solution(mesh):
    nz = mesh.shape["ctx"] // X
    spec = P("ctx", "seq")
    return jax.shard_map(
        functools.partial(body, nz), mesh=mesh, in_specs=(spec,) * 4, out_specs=(spec,) * 4, check_vma=False)
```

time: 391 us -> 55.5 us (0.14)
  the two profiles are of different devices: /device:TPU:1 before, /device:TPU:32 now
where the time goes in v1:
time: 55.5 us; the launch traced here: 55.2 us
  Pallas kernels  47.2 us (85%)
  local copies, waits for them, and re-layouts  7.33 us (13%)
  between operations  0.65 us (1%)
    pallas_call x1, Pallas kernels, body(): pl.pallas_call(functools.partial(kernel, nz, nb), out_shape=(shape,) * 4,...  47.2 us
    unnamed x12, local copies, waits for them, and re-layouts  7.33 us

profile of v1, /device:TPU:32, one launch (start us, length us, event | category | flops | bytes accessed | tf_op | source)
XLA Modules:
  0.0 55.2 jit_solution(10405325691730655045)
XLA Ops:
  0.6 0.0 copy-start
  0.6 1.0 %copy-done = bf16[512,512]{1,0:T(8,128)(2,1)S(1)} copy-done((bf16[512,512]{1,0:T(8,128)(2,1)S(1)}, bf16[512,512]{1,0:T(8,128)(2,1)}, u32[]{:S(2)}) %copy-start) | copy-done | bytes 524312
  1.7 0.0 copy-start.1
  1.7 1.0 %copy-done.1 = bf16[512,512]{1,0:T(8,128)(2,1)S(1)} copy-done((bf16[512,512]{1,0:T(8,128)(2,1)S(1)}, bf16[512,512]{1,0:T(8,128)(2,1)}, u32[]{:S(2)}) %copy-start.1) | copy-done | bytes 524312
  2.7 0.0 copy-start.2
  2.7 1.0 %copy-done.2 = bf16[512,512]{1,0:T(8,128)(2,1)S(1)} copy-done((bf16[512,512]{1,0:T(8,128)(2,1)S(1)}, bf16[512,512]{1,0:T(8,128)(2,1)}, u32[]{:S(2)}) %copy-start.2) | copy-done | bytes 524312
  3.8 0.0 copy-start.3
  3.8 1.0 %copy-done.3 = bf16[512,512]{1,0:T(8,128)(2,1)S(1)} copy-done((bf16[512,512]{1,0:T(8,128)(2,1)S(1)}, bf16[512,512]{1,0:T(8,128)(2,1)}, u32[]{:S(2)}) %copy-start.3) | copy-done | bytes 524312
  4.8 47.2 %shard_map.75 = (bf16[512,512]{1,0:T(8,128)(2,1)S(1)}, bf16[512,512]{1,0:T(8,128)(2,1)S(1)}, bf16[512,512]{1,0:T(8,128)(2,1)S(1)}, bf16[512,512]{1,0:T(8,128)(2,1)S(1)}) custom-call(bf16[512,512]{1,0:T(8,128)(2,1)S(1)} %copy-done, bf16[512,512]{1,0:T(8,128)(2,1)S(1)} %copy-done.1, bf16[512,512]{1,0:T(8,128)(2,1)S(1)} %copy-done.2, bf16[512,512]{1,0:T(8,128)(2,1)S(1)} %copy-done.3), custom_call_target="tpu_custom_call" | custom-call | tf_op jit(solution)/shard_map/pallas_call | solution.py:218
  52.0 0.8 %copy.12 = bf16[512,512]{1,0:T(8,128)(2,1)} copy(bf16[512,512]{1,0:T(8,128)(2,1)S(1)} %get-tuple-element.8) | data formatting | bytes 1048576
  52.8 0.8 %copy.13 = bf16[512,512]{1,0:T(8,128)(2,1)} copy(bf16[512,512]{1,0:T(8,128)(2,1)S(1)} %get-tuple-element.9) | data formatting | bytes 1048576
  53.6 0.8 %copy.14 = bf16[512,512]{1,0:T(8,128)(2,1)} copy(bf16[512,512]{1,0:T(8,128)(2,1)S(1)} %get-tuple-element.10) | data formatting | bytes 1048576
  54.4 0.8 %copy.15 = bf16[512,512]{1,0:T(8,128)(2,1)} copy(bf16[512,512]{1,0:T(8,128)(2,1)S(1)} %get-tuple-element.11) | data formatting | bytes 1048576
Async XLA Ops:
  0.6 1.0 %copy-start = (bf16[512,512]{1,0:T(8,128)(2,1)S(1)}, bf16[512,512]{1,0:T(8,128)(2,1)}, u32[]{:S(2)}) copy-start(bf16[512,512]{1,0:T(8,128)(2,1)} %q_hbm.1) | copy-start | bytes 1572868
  1.7 1.0 %copy-start.1 = (bf16[512,512]{1,0:T(8,128)(2,1)S(1)}, bf16[512,512]{1,0:T(8,128)(2,1)}, u32[]{:S(2)}) copy-start(bf16[512,512]{1,0:T(8,128)(2,1)} %k_hbm.1) | copy-start | bytes 1572868
  2.7 1.0 %copy-start.2 = (bf16[512,512]{1,0:T(8,128)(2,1)S(1)}, bf16[512,512]{1,0:T(8,128)(2,1)}, u32[]{:S(2)}) copy-start(bf16[512,512]{1,0:T(8,128)(2,1)} %v_hbm.1) | copy-start | bytes 1572868
  3.8 1.0 %copy-start.3 = (bf16[512,512]{1,0:T(8,128)(2,1)S(1)}, bf16[512,512]{1,0:T(8,128)(2,1)}, u32[]{:S(2)}) copy-start(bf16[512,512]{1,0:T(8,128)(2,1)} %g_hbm.1) | copy-start | bytes 1572868

commit v2 on v1

v2 whole, which is shorter than its diff:
```python
import functools

import jax
import jax.numpy as jnp
from jax import lax
from jax.experimental import pallas as pl
from jax.experimental.pallas import tpu as pltpu
from jax.sharding import PartitionSpec as P

DH = 128
BLOCK = 128
X = 4
MESH = pl.DeviceIdType.MESH
F32 = jnp.float32
BF16 = jnp.bfloat16


def dot(a, b, ca, cb):
    return lax.dot_general(a, b, (((ca,), (cb,)), ((), ())), preferred_element_type=F32)


def rounds_of(nz):
    known, dists = 1, []
    while known < nz // 2:
        step = min(known, nz // 2 - known)
        dists.append(step)
        known += step
    return dists


def kernel(
    nz, nb, q_hbm, k_hbm, v_hbm, g_hbm, *refs,
):
    outs = refs[:4]
    (qs, ks, vs, gs, cum, part, xsend, xrecv, tbuf, zrecv, zsend, zpre, xback, before,
     in_sem, ring_sem, xu_s, xu_r, zu_s, zu_r, zd_s, zd_r, xd_s, xd_r) = refs[4:]
    rows = tbuf.shape[1] // nz
    c = lax.axis_index("ctx")
    seq = lax.axis_index("seq")
    z = c // X
    x = c % X

    def xdev(d):
        return (z * X + (x + d) % X, seq)

    def zdev(d):
        return (((z + d) % nz) * X + x, seq)

    def both(d):
        return sorted({d, nz - d})

    zorder = sorted(range(1, nz), key=lambda d: -min(d, nz - d))
    rounds = rounds_of(nz)

    loads = {}

    def load(i, hbm, buf):
        cp = pltpu.make_async_copy(hbm, buf, in_sem.at[i])
        cp.start()
        loads[i] = cp

    load(1, k_hbm, ks)
    load(2, v_hbm, vs)
    barrier = pltpu.get_barrier_semaphore()
    for d in (2, 1, 3):
        pl.semaphore_signal(barrier, inc=1, device_id=xdev(d), device_id_type=MESH)
    for d in both(1):
        pl.semaphore_signal(barrier, inc=1, device_id=zdev(d), device_id_type=MESH)
    load(0, q_hbm, qs)
    load(3, g_hbm, gs)

    def ring_signal(i):
        for d in both(rounds[i]):
            pl.semaphore_signal(ring_sem.at[i], inc=1, device_id=zdev(d), device_id_type=MESH)

    def ring_wait(i):
        pl.semaphore_wait(ring_sem.at[i], len(both(rounds[i])))

    def cols(s):
        return pl.ds(pl.multiple_of(((x + s) % X) * DH, DH), DH)

    slots = (2, 1, 3, 0)
    pad = tbuf.shape[1] - DH
    base = (0, pad)
    for kind in range(2):
        if pad:
            lo = DH if kind == 0 else 0
            tbuf[kind, lo:lo + pad, :] = jnp.zeros((pad, DH), F32)

    def local_state(kind, s):
        a, b = ((ks, vs), (qs, gs))[kind]
        run = jnp.zeros((DH, DH), F32)
        for blk in (range(nb) if kind == 0 else range(nb - 1, -1, -1)):
            cum[kind, s, blk] = run
            r = pl.ds(blk * BLOCK, BLOCK)
            run = run + dot(a[r, cols(s)], b[r, cols(s)], 0, 0)
        return run

    for kind in range(2):
        for i in ((1, 2), (0, 3))[kind]:
            loads[i].wait()
        for s in slots:
            total = local_state(kind, s)
            if s == 0:
                xrecv[kind, x] = total
            else:
                xsend[kind, s - 1] = total
                if kind == 0 and s == slots[0]:
                    pl.semaphore_wait(barrier, X - 1 + len(both(1)))
                pltpu.make_async_remote_copy(
                    xsend.at[kind, s - 1], xrecv.at[kind, x], xu_s.at[kind], xu_r.at[kind],
                    device_id=xdev(s), device_id_type=MESH).start()
        if kind == 0 and rounds:
            ring_signal(0)
    for i in range(1, len(rounds)):
        ring_wait(i - 1)
        ring_signal(i)

    tri = (lax.broadcasted_iota(jnp.int32, (BLOCK, BLOCK), 1)
           <= lax.broadcasted_iota(jnp.int32, (BLOCK, BLOCK), 0))

    def intra(s):
        for blk in range(nb):
            r = pl.ds(blk * BLOCK, BLOCK)
            q, k, v, g = qs[r, cols(s)], ks[r, cols(s)], vs[r, cols(s)], gs[r, cols(s)]
            attn = jnp.where(tri, dot(q, k, 1, 1), 0.0).astype(BF16)
            grads = jnp.where(tri, dot(g, v, 1, 1), 0.0).astype(BF16)
            part[0, s, r, :] = dot(attn, v, 1, 0)
            part[1, s, r, :] = dot(grads, k, 1, 0)
            part[2, s, r, :] = dot(grads, q, 0, 0)
            part[3, s, r, :] = dot(attn, g, 0, 0)

    def group(src, dst, send, recv, dev):
        return pltpu.make_async_remote_copy(src, dst, send, recv, device_id=dev, device_id_type=MESH)

    def xup(kind):
        return group(xsend.at[kind], xrecv.at[kind, pl.ds(0, X - 1)], xu_s.at[kind], xu_r.at[kind], xdev(1))

    def zup(kind):
        part_rows = pl.ds(0, nz - 1)
        return group(zsend.at[kind, part_rows], zrecv.at[kind, part_rows], zu_s.at[kind], zu_r.at[kind], zdev(1))

    def zdn(kind):
        part_rows = pl.ds(0, (nz - 1) * rows)
        return group(tbuf.at[kind, part_rows], zpre.at[kind, part_rows], zd_s.at[kind], zd_r.at[kind], zdev(1))

    def xdn(kind):
        return group(xback.at[kind, pl.ds(0, X - 1)], before.at[kind, pl.ds(0, X - 1)], xd_s.at[kind], xd_r.at[kind, 0], xdev(1))

    intra(0)
    for kind in range(2):
        xup(kind).wait_recv()
        total = xrecv[kind, 0]
        for i in range(1, X):
            total = total + xrecv[kind, i]
        tbuf[kind, base[kind]:base[kind] + DH, :] = total
        if kind == 0 and rounds:
            ring_wait(len(rounds) - 1)
        for d in zorder:
            pltpu.make_async_remote_copy(
                tbuf.at[kind, pl.ds(pl.multiple_of(((z + d) % nz) * rows, 8), rows)],
                zrecv.at[kind, z], zu_s.at[kind], zu_r.at[kind],
                device_id=zdev(d), device_id_type=MESH).start()
        zrecv[kind, z] = tbuf[kind, pl.ds(pl.multiple_of(z * rows, 8), rows), :]

    intra(1)
    for kind in range(2):
        zup(kind).wait_recv()
        run = jnp.zeros((rows, DH), F32)
        for i in (range(nz) if kind == 0 else range(nz - 1, -1, -1)):
            zsend[kind, i] = run
            run = run + zrecv[kind, i]
        mine = pl.ds(pl.multiple_of(z * rows, 8), rows)
        for d in zorder:
            pltpu.make_async_remote_copy(
                zsend.at[kind, (z + d) % nz], zpre.at[kind, mine], zd_s.at[kind], zd_r.at[kind],
                device_id=zdev(d), device_id_type=MESH).start()
        zpre[kind, mine, :] = zsend[kind, z]

    intra(2)
    for kind in range(2):
        zdn(kind).wait_recv()
        run = zpre[kind, base[kind]:base[kind] + DH, :]
        for i in (range(X) if kind == 0 else range(X - 1, -1, -1)):
            xback[kind, i] = run
            run = run + xrecv[kind, i]
        for d in (2, 1, 3):
            pltpu.make_async_remote_copy(
                xback.at[kind, (x + d) % X], before.at[kind, X - d], xd_s.at[kind], xd_r.at[kind, d - 1],
                device_id=xdev(d), device_id_type=MESH).start()
        before[kind, 0] = xback[kind, x]

    intra(3)
    for kind in range(2):
        for s in (0, 1, 3, 2):
            if s:
                group(xback.at[kind, 0], before.at[kind, s], xd_s.at[kind], xd_r.at[kind, X - s - 1], xdev(1)).wait_recv()
            for blk in range(nb):
                r = pl.ds(blk * BLOCK, BLOCK)
                low = (before[kind, s] + cum[kind, s, blk]).astype(BF16)
                if kind == 0:
                    first, second = dot(qs[r, cols(s)], low, 1, 0), dot(gs[r, cols(s)], low, 1, 1)
                else:
                    first, second = dot(vs[r, cols(s)], low, 1, 1), dot(ks[r, cols(s)], low, 1, 0)
                outs[2 * kind][r, cols(s)] = (part[2 * kind, s, r, :] + first).astype(BF16)
                outs[2 * kind + 1][r, cols(s)] = (part[2 * kind + 1, s, r, :] + second).astype(BF16)

    for kind in range(2):
        for phase in (xup, zup, zdn, xdn):
            phase(kind).wait_send()


def write_out(*refs):
    sem = refs[8]
    copies = [pltpu.make_async_copy(refs[i], refs[4 + i], sem.at[i]) for i in range(4)]
    for cp in copies:
        cp.start()
    for cp in copies:
        cp.wait()


def body(nz, queries, keys, values, out_grad):
    count, width = queries.shape
    nb = count // BLOCK
    assert width == X * DH
    rows = -(-(DH // 8) // nz) * 8
    hbm = pl.BlockSpec(memory_space=pltpu.HBM)
    vmem = pl.BlockSpec(memory_space=pltpu.VMEM)
    vm = pltpu.VMEM
    dma = pltpu.SemaphoreType.DMA
    shape = jax.ShapeDtypeStruct((count, width), BF16)
    outs = pl.pallas_call(
        functools.partial(kernel, nz, nb),
        out_shape=(pltpu.VMEM((count, width), BF16),) * 4,
        in_specs=[hbm] * 4,
        out_specs=(vmem,) * 4,
        scratch_shapes=[
            vm((count, width), BF16),
            vm((count, width), BF16),
            vm((count, width), BF16),
            vm((count, width), BF16),
            vm((2, X, nb, DH, DH), F32),
            vm((4, X, count, DH), F32),
            vm((2, X - 1, DH, DH), F32),
            vm((2, X, DH, DH), F32),
            vm((2, nz * rows, DH), F32),
            vm((2, nz, rows, DH), F32),
            vm((2, nz, rows, DH), F32),
            vm((2, nz * rows, DH), F32),
            vm((2, X, DH, DH), F32),
            vm((2, X, DH, DH), F32),
            dma((4,)),
            pltpu.SemaphoreType.REGULAR((max(1, len(rounds_of(nz))),)),
            dma((2,)), dma((2,)),
            dma((2,)), dma((2,)),
            dma((2,)), dma((2,)),
            dma((2,)), dma((2, X - 1)),
        ],
        compiler_params=pltpu.CompilerParams(
            collective_id=0, has_side_effects=True, vmem_limit_bytes=32 * 1024 * 1024),
    )(*(pltpu.with_memory_space_constraint(a, pltpu.HBM) for a in (queries, keys, values, out_grad)))
    return pl.pallas_call(
        write_out,
        out_shape=(shape,) * 4,
        in_specs=[vmem] * 4,
        out_specs=(hbm,) * 4,
        scratch_shapes=[dma((4,))],
    )(*(pltpu.with_memory_space_constraint(a, pltpu.VMEM) for a in outs))


def solution(mesh):
    nz = mesh.shape["ctx"] // X
    spec = P("ctx", "seq")
    return jax.shard_map(
        functools.partial(body, nz), mesh=mesh, in_specs=(spec,) * 4, out_specs=(spec,) * 4, check_vma=False)
```

time: 55.5 us -> 44 us (0.79)
  the two profiles are of different devices: /device:TPU:32 before, /device:TPU:16 now
where the time goes in v2:
time: 44 us; the launch traced here: 43.9 us
  Pallas kernels  43.2 us (98%)
  between operations  0.64 us (1%)
    pallas_call x1, Pallas kernels, body(): pl.pallas_call(functools.partial(kernel, nz, nb), out_shape=(pltpu.VMEM((...  41.9 us
    pallas_call x1, Pallas kernels, body(): pl.pallas_call(write_out, out_shape=(shape,) * 4, in_specs=[vmem] * 4, ou...  1.35 us

profile of v2, /device:TPU:16, one launch (start us, length us, event | category | flops | bytes accessed | tf_op | source)
XLA Modules:
  0.0 43.9 jit_solution(6230341211673812081)
XLA Ops:
  0.6 41.9 %shard_map.75 = (bf16[512,512]{1,0:T(8,128)(2,1)S(1)}, bf16[512,512]{1,0:T(8,128)(2,1)S(1)}, bf16[512,512]{1,0:T(8,128)(2,1)S(1)}, bf16[512,512]{1,0:T(8,128)(2,1)S(1)}) custom-call(bf16[512,512]{1,0:T(8,128)(2,1)} %q_hbm.1, bf16[512,512]{1,0:T(8,128)(2,1)} %k_hbm.1, bf16[512,512]{1,0:T(8,128)(2,1)} %v_hbm.1, bf16[512,512]{1,0:T(8,128)(2,1)} %g_hbm.1), custom_call_target="tpu_custom_call" | custom-call | tf_op jit(solution)/shard_map/pallas_call | solution.py:232
  42.5 1.3 %shard_map.76 = (bf16[512,512]{1,0:T(8,128)(2,1)}, bf16[512,512]{1,0:T(8,128)(2,1)}, bf16[512,512]{1,0:T(8,128)(2,1)}, bf16[512,512]{1,0:T(8,128)(2,1)}) custom-call(bf16[512,512]{1,0:T(8,128)(2,1)S(1)} %get-tuple-element.8.refs_0_, bf16[512,512]{1,0:T(8,128)(2,1)S(1)} %get-tuple-element.9.refs_1_, bf16[512,512]{1,0:T(8,128)(2,1)S(1)} %get-tuple-element.10.refs_2_, ...), custom_call_target="tpu_custom_call" | custom-call | tf_op jit(solution)/shard_map/pallas_call | solution.py:262

commit v3 on v2

v3 whole, which is shorter than its diff:
```python
import functools

import jax
import jax.numpy as jnp
from jax import lax
from jax.experimental import pallas as pl
from jax.experimental.pallas import tpu as pltpu
from jax.sharding import PartitionSpec as P

DH = 128
BLOCK = 128
X = 4
HALVES = 2
HALF = DH // HALVES
CHUNKS = tuple((kind, half) for kind in range(2) for half in range(HALVES))
MESH = pl.DeviceIdType.MESH
F32 = jnp.float32
BF16 = jnp.bfloat16


def dot(a, b, ca, cb):
    return lax.dot_general(a, b, (((ca,), (cb,)), ((), ())), preferred_element_type=F32)


def rounds_of(nz):
    known, dists = 1, []
    while known < nz // 2:
        step = min(known, nz // 2 - known)
        dists.append(step)
        known += step
    return dists


def kernel(
    nz, nb, q_hbm, k_hbm, v_hbm, g_hbm, *refs,
):
    outs = refs[:4]
    (qs, ks, vs, gs, cum, part, xsend, xrecv, tbuf, zrecv, zsend, zpre, xback, before,
     in_sem, kv_sem, ring_sem, xu_s, xu_r, zu_s, zu_r, zd_s, zd_r, xd_s, xd_r) = refs[4:]
    owners = 2 * nz // 3
    rows = HALF // owners
    c = lax.axis_index("ctx")
    seq = lax.axis_index("seq")
    z = c // X
    x = c % X

    def xdev(d):
        return (z * X + (x + d) % X, seq)

    def zdev(d):
        return (((z + d) % nz) * X + x, seq)

    def both(d):
        return sorted({d, nz - d})

    def owns(n, at):
        return at % 3 != (2, 0, 1, 2)[n % 4]

    def owned(n, at):
        place = (at % 3, at % 3 - 1, (at % 3) // 2, at % 3)[n % 4]
        return pl.ds(pl.multiple_of((n % HALVES) * HALF + ((at // 3) * 2 + place) * rows, 8), rows)

    def half_rows(half):
        return pl.ds(half * HALF, HALF)

    zorder = sorted(range(1, nz), key=lambda d: -min(d, nz - d))
    rounds = rounds_of(nz)

    def cols(s):
        return pl.ds(pl.multiple_of(((x + s) % X) * DH, DH), DH)

    slots = (2, 1, 3, 0)
    loads = {}

    def load(i, hbm, buf):
        cp = pltpu.make_async_copy(hbm, buf, in_sem.at[i])
        cp.start()
        loads[i] = cp

    for s in slots:
        for i, hbm, buf in ((1, k_hbm, ks), (2, v_hbm, vs)):
            cp = pltpu.make_async_copy(hbm.at[:, cols(s)], buf.at[:, cols(s)], kv_sem.at[i - 1, s])
            cp.start()
            loads[i, s] = cp
    barrier = pltpu.get_barrier_semaphore()
    for d in (2, 1, 3):
        pl.semaphore_signal(barrier, inc=1, device_id=xdev(d), device_id_type=MESH)
    for d in both(1):
        pl.semaphore_signal(barrier, inc=1, device_id=zdev(d), device_id_type=MESH)
    load(0, q_hbm, qs)
    load(3, g_hbm, gs)

    def ring_signal(i):
        for d in both(rounds[i]):
            pl.semaphore_signal(ring_sem.at[i], inc=1, device_id=zdev(d), device_id_type=MESH)

    def ring_wait(i):
        pl.semaphore_wait(ring_sem.at[i], len(both(rounds[i])))

    def local_state(kind, s):
        a, b = ((ks, vs), (qs, gs))[kind]
        run = jnp.zeros((DH, DH), F32)
        for blk in (range(nb) if kind == 0 else range(nb - 1, -1, -1)):
            cum[kind, s, blk] = run
            r = pl.ds(blk * BLOCK, BLOCK)
            run = run + dot(a[r, cols(s)], b[r, cols(s)], 0, 0)
        return run

    def send_state(kind, s, half):
        n = kind * HALVES + half
        pltpu.make_async_remote_copy(
            xsend.at[kind, s - 1, half_rows(half)], xrecv.at[kind, x, half_rows(half)], xu_s.at[n], xu_r.at[n],
            device_id=xdev(s), device_id_type=MESH).start()

    for kind in range(2):
        if kind == 1:
            loads[0].wait()
            loads[3].wait()
        for s in slots:
            if kind == 0:
                loads[1, s].wait()
                loads[2, s].wait()
            total = local_state(kind, s)
            if s == 0:
                xrecv[kind, x] = total
            else:
                xsend[kind, s - 1] = total
                if kind == 0 and s == slots[0]:
                    pl.semaphore_wait(barrier, X - 1 + len(both(1)))
                send_state(kind, s, 0)
        for half in range(1, HALVES):
            for s in slots[:-1]:
                send_state(kind, s, half)
        if kind == 0 and rounds:
            ring_signal(0)
    for i in range(1, len(rounds)):
        ring_wait(i - 1)
        ring_signal(i)

    tri = (lax.broadcasted_iota(jnp.int32, (BLOCK, BLOCK), 1)
           <= lax.broadcasted_iota(jnp.int32, (BLOCK, BLOCK), 0))

    def intra(s):
        for blk in range(nb):
            r = pl.ds(blk * BLOCK, BLOCK)
            q, k, v, g = qs[r, cols(s)], ks[r, cols(s)], vs[r, cols(s)], gs[r, cols(s)]
            attn = jnp.where(tri, dot(q, k, 1, 1), 0.0).astype(BF16)
            grads = jnp.where(tri, dot(g, v, 1, 1), 0.0).astype(BF16)
            part[0, s, r, :] = dot(attn, v, 1, 0)
            part[1, s, r, :] = dot(grads, k, 1, 0)
            part[2, s, r, :] = dot(grads, q, 0, 0)
            part[3, s, r, :] = dot(attn, g, 0, 0)

    def group(src, dst, send, recv, dev):
        return pltpu.make_async_remote_copy(src, dst, send, recv, device_id=dev, device_id_type=MESH)

    def xup(n):
        kind, half = CHUNKS[n]
        return group(xsend.at[kind, pl.ds(0, X - 1), half_rows(half)], xrecv.at[kind, pl.ds(0, X - 1), half_rows(half)],
                     xu_s.at[n], xu_r.at[n], xdev(1))

    def zup(n, count):
        return group(zsend.at[n, pl.ds(0, count)], zrecv.at[n, pl.ds(0, count)], zu_s.at[n], zu_r.at[n], zdev(1))

    def zdn(n, count):
        return group(zsend.at[n, pl.ds(0, count)], zrecv.at[n, pl.ds(0, count)], zd_s.at[n], zd_r.at[n], zdev(1))

    def xdn(n, count, d):
        kind, half = CHUNKS[n]
        return group(xback.at[kind, pl.ds(0, count), half_rows(half)], before.at[kind, pl.ds(0, count), half_rows(half)],
                     xd_s.at[n], xd_r.at[n, d - 1], xdev(1))

    intra(0)
    for n, (kind, half) in enumerate(CHUNKS):
        xup(n).wait_recv()
        total = xrecv[kind, 0, half_rows(half), :]
        for i in range(1, X):
            total = total + xrecv[kind, i, half_rows(half), :]
        tbuf[kind, half_rows(half), :] = total
        if n == 0 and rounds:
            ring_wait(len(rounds) - 1)
        for d in zorder:
            to = (z + d) % nz

            @pl.when(owns(n, to))
            def _(n=n, kind=kind, d=d, to=to):
                pltpu.make_async_remote_copy(
                    tbuf.at[kind, owned(n, to)], zrecv.at[n, z], zu_s.at[n], zu_r.at[n],
                    device_id=zdev(d), device_id_type=MESH).start()

    intra(1)
    for n, (kind, half) in enumerate(CHUNKS):

        @pl.when(owns(n, z))
        def _(n=n, kind=kind):
            mine = owned(n, z)
            zrecv[n, z] = tbuf[kind, mine, :]
            zup(n, nz - 1).wait_recv()
            run = jnp.zeros((rows, DH), F32)
            for i in (range(nz) if kind == 0 else range(nz - 1, -1, -1)):
                zsend[n, i] = run
                run = run + zrecv[n, i]
            for d in zorder:
                pltpu.make_async_remote_copy(
                    zsend.at[n, (z + d) % nz], zpre.at[kind, mine], zd_s.at[n], zd_r.at[n],
                    device_id=zdev(d), device_id_type=MESH).start()
            zpre[kind, mine, :] = zsend[n, z]

    intra(2)
    for n, (kind, half) in enumerate(CHUNKS):
        @pl.when(owns(n, z))
        def _(n=n):
            zdn(n, owners - 1).wait_recv()

        @pl.when(jnp.logical_not(owns(n, z)))
        def _(n=n):
            zdn(n, owners).wait_recv()

        run = zpre[kind, half_rows(half), :]
        for i in (range(X) if kind == 0 else range(X - 1, -1, -1)):
            xback[kind, i, half_rows(half), :] = run
            run = run + xrecv[kind, i, half_rows(half), :]
        for d in (2, 1, 3):
            pltpu.make_async_remote_copy(
                xback.at[kind, (x + d) % X, half_rows(half)], before.at[kind, X - d, half_rows(half)],
                xd_s.at[n], xd_r.at[n, d - 1], device_id=xdev(d), device_id_type=MESH).start()
        before[kind, 0, half_rows(half), :] = xback[kind, x, half_rows(half), :]

    intra(3)
    for kind in range(2):
        for s in (0, 1, 3, 2):
            if s:
                for half in range(HALVES):
                    xdn(kind * HALVES + half, 1, X - s).wait_recv()
            for blk in range(nb):
                r = pl.ds(blk * BLOCK, BLOCK)
                low = (before[kind, s] + cum[kind, s, blk]).astype(BF16)
                if kind == 0:
                    first, second = dot(qs[r, cols(s)], low, 1, 0), dot(gs[r, cols(s)], low, 1, 1)
                else:
                    first, second = dot(vs[r, cols(s)], low, 1, 1), dot(ks[r, cols(s)], low, 1, 0)
                outs[2 * kind][r, cols(s)] = (part[2 * kind, s, r, :] + first).astype(BF16)
                outs[2 * kind + 1][r, cols(s)] = (part[2 * kind + 1, s, r, :] + second).astype(BF16)

    for n in range(len(CHUNKS)):
        xup(n).wait_send()

        @pl.when(owns(n, z))
        def _(n=n):
            zup(n, owners - 1).wait_send()
            zdn(n, nz - 1).wait_send()

        @pl.when(jnp.logical_not(owns(n, z)))
        def _(n=n):
            zup(n, owners).wait_send()

        xdn(n, X - 1, 1).wait_send()


def write_out(*refs):
    sem = refs[8]
    copies = [pltpu.make_async_copy(refs[i], refs[4 + i], sem.at[i]) for i in range(4)]
    for cp in copies:
        cp.start()
    for cp in copies:
        cp.wait()


def body(nz, queries, keys, values, out_grad):
    count, width = queries.shape
    nb = count // BLOCK
    assert width == X * DH
    assert nz % 3 == 0 and HALF * 3 % (2 * nz) == 0
    rows = HALF * 3 // (2 * nz)
    nc = len(CHUNKS)
    hbm = pl.BlockSpec(memory_space=pltpu.HBM)
    vmem = pl.BlockSpec(memory_space=pltpu.VMEM)
    vm = pltpu.VMEM
    dma = pltpu.SemaphoreType.DMA
    shape = jax.ShapeDtypeStruct((count, width), BF16)
    outs = pl.pallas_call(
        functools.partial(kernel, nz, nb),
        out_shape=(pltpu.VMEM((count, width), BF16),) * 4,
        in_specs=[hbm] * 4,
        out_specs=(vmem,) * 4,
        scratch_shapes=[
            vm((count, width), BF16),
            vm((count, width), BF16),
            vm((count, width), BF16),
            vm((count, width), BF16),
            vm((2, X, nb, DH, DH), F32),
            vm((4, X, count, DH), F32),
            vm((2, X - 1, DH, DH), F32),
            vm((2, X, DH, DH), F32),
            vm((2, DH, DH), F32),
            vm((nc, nz, rows, DH), F32),
            vm((nc, nz, rows, DH), F32),
            vm((2, DH, DH), F32),
            vm((2, X, DH, DH), F32),
            vm((2, X, DH, DH), F32),
            dma((4,)), dma((2, X)),
            pltpu.SemaphoreType.REGULAR((max(1, len(rounds_of(nz))),)),
            dma((nc,)), dma((nc,)),
            dma((nc,)), dma((nc,)),
            dma((nc,)), dma((nc,)),
            dma((nc,)), dma((nc, X - 1)),
        ],
        compiler_params=pltpu.CompilerParams(
            collective_id=0, has_side_effects=True, vmem_limit_bytes=32 * 1024 * 1024),
    )(*(pltpu.with_memory_space_constraint(a, pltpu.HBM) for a in (queries, keys, values, out_grad)))
    return pl.pallas_call(
        write_out,
        out_shape=(shape,) * 4,
        in_specs=[vmem] * 4,
        out_specs=(hbm,) * 4,
        scratch_shapes=[dma((4,))],
    )(*(pltpu.with_memory_space_constraint(a, pltpu.VMEM) for a in outs))


def solution(mesh):
    nz = mesh.shape["ctx"] // X
    spec = P("ctx", "seq")
    return jax.shard_map(
        functools.partial(body, nz), mesh=mesh, in_specs=(spec,) * 4, out_specs=(spec,) * 4, check_vma=False)
```

time: 44 us -> 41.7 us (0.948)
  the two profiles are of different devices: /device:TPU:16 before, /device:TPU:48 now
where the time goes in v3:
time: 41.7 us; the launch traced here: 41.5 us
  Pallas kernels  40.9 us (98%)
  between operations  0.64 us (2%)
    pallas_call x1, Pallas kernels, body(): pl.pallas_call(functools.partial(kernel, nz, nb), out_shape=(pltpu.VMEM((...  39.5 us
    pallas_call x1, Pallas kernels, body(): pl.pallas_call(write_out, out_shape=(shape,) * 4, in_specs=[vmem] * 4, ou...  1.35 us

profile of v3, /device:TPU:48, one launch (start us, length us, event | category | flops | bytes accessed | tf_op | source)
XLA Modules:
  0.0 41.5 jit_solution(17509378557273258113)
XLA Ops:
  0.6 39.5 %shard_map.75 = (bf16[512,512]{1,0:T(8,128)(2,1)S(1)}, bf16[512,512]{1,0:T(8,128)(2,1)S(1)}, bf16[512,512]{1,0:T(8,128)(2,1)S(1)}, bf16[512,512]{1,0:T(8,128)(2,1)S(1)}) custom-call(bf16[512,512]{1,0:T(8,128)(2,1)} %q_hbm.1, bf16[512,512]{1,0:T(8,128)(2,1)} %k_hbm.1, bf16[512,512]{1,0:T(8,128)(2,1)} %v_hbm.1, bf16[512,512]{1,0:T(8,128)(2,1)} %g_hbm.1), custom_call_target="tpu_custom_call" | custom-call | tf_op jit(solution)/shard_map/pallas_call | solution.py:281
  40.2 1.3 %shard_map.76 = (bf16[512,512]{1,0:T(8,128)(2,1)}, bf16[512,512]{1,0:T(8,128)(2,1)}, bf16[512,512]{1,0:T(8,128)(2,1)}, bf16[512,512]{1,0:T(8,128)(2,1)}) custom-call(bf16[512,512]{1,0:T(8,128)(2,1)S(1)} %get-tuple-element.8.refs_0_, bf16[512,512]{1,0:T(8,128)(2,1)S(1)} %get-tuple-element.9.refs_1_, bf16[512,512]{1,0:T(8,128)(2,1)S(1)} %get-tuple-element.10.refs_2_, ...), custom_call_target="tpu_custom_call" | custom-call | tf_op jit(solution)/shard_map/pallas_call | solution.py:311

commit v4 on v3

--- a/solution.py
+++ b/solution.py
@@ -13,6 +13,7 @@
 HALVES = 2
 HALF = DH // HALVES
 CHUNKS = tuple((kind, half) for kind in range(2) for half in range(HALVES))
+LATE_FIRST = tuple(sorted(range(len(CHUNKS)), key=lambda n: -CHUNKS[n][0]))
 MESH = pl.DeviceIdType.MESH
 F32 = jnp.float32
 BF16 = jnp.bfloat16
@@ -36,8 +37,9 @@
 ):
     outs = refs[:4]
     (qs, ks, vs, gs, cum, part, xsend, xrecv, tbuf, zrecv, zsend, zpre, xback, before,
-     in_sem, kv_sem, ring_sem, xu_s, xu_r, zu_s, zu_r, zd_s, zd_r, xd_s, xd_r) = refs[4:]
+     in_sem, qg_sem, ring_sem, xu_s, xu_r, zu_s, zu_r, zk_r, zd_s, zd_r, xd_s, xd_r) = refs[4:]
     owners = 2 * nz // 3
+    early = nz // 3
     rows = HALF // owners
     c = lax.axis_index("ctx")
     seq = lax.axis_index("seq")
@@ -60,6 +62,9 @@
         place = (at % 3, at % 3 - 1, (at % 3) // 2, at % 3)[n % 4]
         return pl.ds(pl.multiple_of((n % HALVES) * HALF + ((at // 3) * 2 + place) * rows, 8), rows)
 
+    def arrival(n):
+        return zk_r.at[n, jnp.minimum(z, early)] if CHUNKS[n][0] == 0 else zu_r.at[n]
+
     def half_rows(half):
         return pl.ds(half * HALF, HALF)
 
@@ -78,8 +83,8 @@
         loads[i] = cp
 
     for s in slots:
-        for i, hbm, buf in ((1, k_hbm, ks), (2, v_hbm, vs)):
-            cp = pltpu.make_async_copy(hbm.at[:, cols(s)], buf.at[:, cols(s)], kv_sem.at[i - 1, s])
+        for i, hbm, buf in ((0, q_hbm, qs), (1, g_hbm, gs)):
+            cp = pltpu.make_async_copy(hbm.at[:, cols(s)], buf.at[:, cols(s)], qg_sem.at[i, s])
             cp.start()
             loads[i, s] = cp
     barrier = pltpu.get_barrier_semaphore()
@@ -87,8 +92,8 @@
         pl.semaphore_signal(barrier, inc=1, device_id=xdev(d), device_id_type=MESH)
     for d in both(1):
         pl.semaphore_signal(barrier, inc=1, device_id=zdev(d), device_id_type=MESH)
-    load(0, q_hbm, qs)
-    load(3, g_hbm, gs)
+    load(0, k_hbm, ks)
+    load(1, v_hbm, vs)
 
     def ring_signal(i):
         for d in both(rounds[i]):
@@ -112,26 +117,26 @@
             xsend.at[kind, s - 1, half_rows(half)], xrecv.at[kind, x, half_rows(half)], xu_s.at[n], xu_r.at[n],
             device_id=xdev(s), device_id_type=MESH).start()
 
-    for kind in range(2):
-        if kind == 1:
+    for kind in (1, 0):
+        if kind == 0:
             loads[0].wait()
-            loads[3].wait()
+            loads[1].wait()
         for s in slots:
-            if kind == 0:
+            if kind == 1:
+                loads[0, s].wait()
                 loads[1, s].wait()
-                loads[2, s].wait()
             total = local_state(kind, s)
             if s == 0:
                 xrecv[kind, x] = total
             else:
                 xsend[kind, s - 1] = total
-                if kind == 0 and s == slots[0]:
+                if kind == 1 and s == slots[0]:
                     pl.semaphore_wait(barrier, X - 1 + len(both(1)))
                 send_state(kind, s, 0)
         for half in range(1, HALVES):
             for s in slots[:-1]:
                 send_state(kind, s, half)
-        if kind == 0 and rounds:
+        if kind == 1 and rounds:
             ring_signal(0)
     for i in range(1, len(rounds)):
         ring_wait(i - 1)
@@ -171,13 +176,14 @@
                      xd_s.at[n], xd_r.at[n, d - 1], xdev(1))
 
     intra(0)
-    for n, (kind, half) in enumerate(CHUNKS):
+    for n in LATE_FIRST:
+        kind, half = CHUNKS[n]
         xup(n).wait_recv()
         total = xrecv[kind, 0, half_rows(half), :]
         for i in range(1, X):
             total = total + xrecv[kind, i, half_rows(half), :]
         tbuf[kind, half_rows(half), :] = total
-        if n == 0 and rounds:
+        if n == LATE_FIRST[0] and rounds:
             ring_wait(len(rounds) - 1)
         for d in zorder:
             to = (z + d) % nz
@@ -185,26 +191,72 @@
             @pl.when(owns(n, to))
             def _(n=n, kind=kind, d=d, to=to):
                 pltpu.make_async_remote_copy(
-                    tbuf.at[kind, owned(n, to)], zrecv.at[n, z], zu_s.at[n], zu_r.at[n],
+                    tbuf.at[kind, owned(n, to)], zrecv.at[n, z], zu_s.at[n], arrival(n),
                     device_id=zdev(d), device_id_type=MESH).start()
 
+    def give(n, to):
+        kind = CHUNKS[n][0]
+
+        @pl.when(z != to)
+        def _():
+            pltpu.make_async_remote_copy(
+                zsend.at[n, to], zpre.at[kind, owned(n, z)], zd_s.at[n], zd_r.at[n],
+                device_id=(to * X + x, seq), device_id_type=MESH).start()
+
+        @pl.when(z == to)
+        def _():
+            zpre[kind, owned(n, z), :] = zsend[n, to]
+
+    def arrived(n, sem, count):
+        group(zsend.at[n, pl.ds(0, count)], zrecv.at[n, pl.ds(0, count)], zd_s.at[n], sem, zdev(1)).wait_recv()
+
+    def scan_early(n):
+        zrecv[n, z] = tbuf[0, owned(n, z), :]
+        run = jnp.zeros((rows, DH), F32)
+        for i in range(early + 1):
+            zsend[n, i] = run
+            give(n, i)
+            if i < early:
+                @pl.when(z != i)
+                def _(i=i):
+                    arrived(n, zk_r.at[n, i], 1)
+
+                run = run + zrecv[n, i]
+
+    def scan_late(n):
+        @pl.when(z < early)
+        def _():
+            arrived(n, zk_r.at[n, early], nz - early)
+
+        @pl.when(z >= early)
+        def _():
+            arrived(n, zk_r.at[n, early], nz - early - 1)
+
+        run = zsend[n, early]
+        for i in range(early, nz - 1):
+            run = run + zrecv[n, i]
+            zsend[n, i + 1] = run
+        for i in range(early + 1, nz):
+            give(n, i)
+
+    def scan_back(n):
+        zrecv[n, z] = tbuf[1, owned(n, z), :]
+        arrived(n, zu_r.at[n], nz - 1)
+        run = jnp.zeros((rows, DH), F32)
+        for i in range(nz - 1, -1, -1):
+            zsend[n, i] = run
+            run = run + zrecv[n, i]
+        for i in range(nz):
+            give(n, i)
+
     intra(1)
-    for n, (kind, half) in enumerate(CHUNKS):
-
-        @pl.when(owns(n, z))
-        def _(n=n, kind=kind):
-            mine = owned(n, z)
-            zrecv[n, z] = tbuf[kind, mine, :]
-            zup(n, nz - 1).wait_recv()
-            run = jnp.zeros((rows, DH), F32)
-            for i in (range(nz) if kind == 0 else range(nz - 1, -1, -1)):
-                zsend[n, i] = run
-                run = run + zrecv[n, i]
-            for d in zorder:
-                pltpu.make_async_remote_copy(
-                    zsend.at[n, (z + d) % nz], zpre.at[kind, mine], zd_s.at[n], zd_r.at[n],
-                    device_id=zdev(d), device_id_type=MESH).start()
-            zpre[kind, mine, :] = zsend[n, z]
+    for scan, kind in ((scan_early, 0), (scan_back, 1), (scan_late, 0)):
+        for half in range(HALVES):
+            n = kind * HALVES + half
+
+            @pl.when(owns(n, z))
+            def _(scan=scan, n=n):
+                scan(n)
 
     intra(2)
     for n, (kind, half) in enumerate(CHUNKS):
@@ -298,10 +350,10 @@
             vm((2, DH, DH), F32),
             vm((2, X, DH, DH), F32),
             vm((2, X, DH, DH), F32),
-            dma((4,)), dma((2, X)),
+            dma((2,)), dma((2, X)),
             pltpu.SemaphoreType.REGULAR((max(1, len(rounds_of(nz))),)),
             dma((nc,)), dma((nc,)),
-            dma((nc,)), dma((nc,)),
+            dma((nc,)), dma((nc,)), dma((HALVES, nz // 3 + 1)),
             dma((nc,)), dma((nc,)),
             dma((nc,)), dma((nc, X - 1)),
         ],

time: 41.7 us -> 41.7 us (level)
  the two profiles are of different devices: /device:TPU:48 before, /device:TPU:8 now
where the time goes in v4:
time: 41.7 us; the launch traced here: 41.6 us
  Pallas kernels  40.9 us (98%)
  between operations  0.64 us (2%)
    pallas_call x1, Pallas kernels, body(): pl.pallas_call(functools.partial(kernel, nz, nb), out_shape=(pltpu.VMEM((...  39.6 us
    pallas_call x1, Pallas kernels, body(): pl.pallas_call(write_out, out_shape=(shape,) * 4, in_specs=[vmem] * 4, ou...  1.35 us

profile of v4, /device:TPU:8, one launch (start us, length us, event | category | flops | bytes accessed | tf_op | source)
XLA Modules:
  0.0 41.6 jit_solution(9650739410651612993)
XLA Ops:
  0.6 39.6 %shard_map.75 = (bf16[512,512]{1,0:T(8,128)(2,1)S(1)}, bf16[512,512]{1,0:T(8,128)(2,1)S(1)}, bf16[512,512]{1,0:T(8,128)(2,1)S(1)}, bf16[512,512]{1,0:T(8,128)(2,1)S(1)}) custom-call(bf16[512,512]{1,0:T(8,128)(2,1)} %q_hbm.1, bf16[512,512]{1,0:T(8,128)(2,1)} %k_hbm.1, bf16[512,512]{1,0:T(8,128)(2,1)} %v_hbm.1, bf16[512,512]{1,0:T(8,128)(2,1)} %g_hbm.1), custom_call_target="tpu_custom_call" | custom-call | tf_op jit(solution)/shard_map/pallas_call | solution.py:333
  40.2 1.3 %shard_map.76 = (bf16[512,512]{1,0:T(8,128)(2,1)}, bf16[512,512]{1,0:T(8,128)(2,1)}, bf16[512,512]{1,0:T(8,128)(2,1)}, bf16[512,512]{1,0:T(8,128)(2,1)}) custom-call(bf16[512,512]{1,0:T(8,128)(2,1)S(1)} %get-tuple-element.8.refs_0_, bf16[512,512]{1,0:T(8,128)(2,1)S(1)} %get-tuple-element.9.refs_1_, bf16[512,512]{1,0:T(8,128)(2,1)S(1)} %get-tuple-element.10.refs_2_, ...), custom_call_target="tpu_custom_call" | custom-call | tf_op jit(solution)/shard_map/pallas_call | solution.py:363

commit v5 on v4

--- a/solution.py
+++ b/solution.py
@@ -11,6 +11,7 @@
 BLOCK = 128
 X = 4
 HALVES = 2
+NEAR = 2
 HALF = DH // HALVES
 CHUNKS = tuple((kind, half) for kind in range(2) for half in range(HALVES))
 LATE_FIRST = tuple(sorted(range(len(CHUNKS)), key=lambda n: -CHUNKS[n][0]))
@@ -24,7 +25,7 @@
 
 
 def rounds_of(nz):
-    known, dists = 1, []
+    known, dists = min(NEAR, nz // 2), []
     while known < nz // 2:
         step = min(known, nz // 2 - known)
         dists.append(step)
@@ -68,6 +69,7 @@
     def half_rows(half):
         return pl.ds(half * HALF, HALF)
 
+    near = sorted({e for d in range(1, min(NEAR, nz // 2) + 1) for e in both(d)})
     zorder = sorted(range(1, nz), key=lambda d: -min(d, nz - d))
     rounds = rounds_of(nz)
 
@@ -90,7 +92,7 @@
     barrier = pltpu.get_barrier_semaphore()
     for d in (2, 1, 3):
         pl.semaphore_signal(barrier, inc=1, device_id=xdev(d), device_id_type=MESH)
-    for d in both(1):
+    for d in near:
         pl.semaphore_signal(barrier, inc=1, device_id=zdev(d), device_id_type=MESH)
     load(0, k_hbm, ks)
     load(1, v_hbm, vs)
@@ -131,13 +133,13 @@
             else:
                 xsend[kind, s - 1] = total
                 if kind == 1 and s == slots[0]:
-                    pl.semaphore_wait(barrier, X - 1 + len(both(1)))
+                    pl.semaphore_wait(barrier, X - 1 + len(near))
+                    if rounds:
+                        ring_signal(0)
                 send_state(kind, s, 0)
         for half in range(1, HALVES):
             for s in slots[:-1]:
                 send_state(kind, s, half)
-        if kind == 1 and rounds:
-            ring_signal(0)
     for i in range(1, len(rounds)):
         ring_wait(i - 1)
         ring_signal(i)

time: 41.7 us -> 41.9 us (level)
  the two profiles are of different devices: /device:TPU:8 before, /device:TPU:16 now
where the time goes in v5:
time: 41.9 us; the launch traced here: 41.8 us
  Pallas kernels  41.1 us (98%)
  between operations  0.64 us (2%)
    pallas_call x1, Pallas kernels, body(): pl.pallas_call(functools.partial(kernel, nz, nb), out_shape=(pltpu.VMEM((...  39.8 us
    pallas_call x1, Pallas kernels, body(): pl.pallas_call(write_out, out_shape=(shape,) * 4, in_specs=[vmem] * 4, ou...  1.35 us

profile of v5, /device:TPU:16, one launch (start us, length us, event | category | flops | bytes accessed | tf_op | source)
XLA Modules:
  0.0 41.8 jit_solution(15607619091385407212)
XLA Ops:
  0.6 39.8 %shard_map.75 = (bf16[512,512]{1,0:T(8,128)(2,1)S(1)}, bf16[512,512]{1,0:T(8,128)(2,1)S(1)}, bf16[512,512]{1,0:T(8,128)(2,1)S(1)}, bf16[512,512]{1,0:T(8,128)(2,1)S(1)}) custom-call(bf16[512,512]{1,0:T(8,128)(2,1)} %q_hbm.1, bf16[512,512]{1,0:T(8,128)(2,1)} %k_hbm.1, bf16[512,512]{1,0:T(8,128)(2,1)} %v_hbm.1, bf16[512,512]{1,0:T(8,128)(2,1)} %g_hbm.1), custom_call_target="tpu_custom_call" | custom-call | tf_op jit(solution)/shard_map/pallas_call | solution.py:335
  40.4 1.3 %shard_map.76 = (bf16[512,512]{1,0:T(8,128)(2,1)}, bf16[512,512]{1,0:T(8,128)(2,1)}, bf16[512,512]{1,0:T(8,128)(2,1)}, bf16[512,512]{1,0:T(8,128)(2,1)}) custom-call(bf16[512,512]{1,0:T(8,128)(2,1)S(1)} %get-tuple-element.8.refs_0_, bf16[512,512]{1,0:T(8,128)(2,1)S(1)} %get-tuple-element.9.refs_1_, bf16[512,512]{1,0:T(8,128)(2,1)S(1)} %get-tuple-element.10.refs_2_, ...), custom_call_target="tpu_custom_call" | custom-call | tf_op jit(solution)/shard_map/pallas_call | solution.py:365

commit v6 on v4

--- a/solution.py
+++ b/solution.py
@@ -82,16 +82,20 @@
         cp.start()
         loads[i] = cp
 
-    for s in slots:
+    def load_head(s):
         for i, hbm, buf in ((0, q_hbm, qs), (1, g_hbm, gs)):
             cp = pltpu.make_async_copy(hbm.at[:, cols(s)], buf.at[:, cols(s)], qg_sem.at[i, s])
             cp.start()
             loads[i, s] = cp
+
+    load_head(slots[0])
     barrier = pltpu.get_barrier_semaphore()
     for d in (2, 1, 3):
         pl.semaphore_signal(barrier, inc=1, device_id=xdev(d), device_id_type=MESH)
     for d in both(1):
         pl.semaphore_signal(barrier, inc=1, device_id=zdev(d), device_id_type=MESH)
+    for s in slots[1:]:
+        load_head(s)
     load(0, k_hbm, ks)
     load(1, v_hbm, vs)
 
@@ -311,7 +315,11 @@
 
 def write_out(*refs):
     sem = refs[8]
-    copies = [pltpu.make_async_copy(refs[i], refs[4 + i], sem.at[i]) for i in range(4)]
+    half = refs[0].shape[0] // 2
+    copies = [
+        pltpu.make_async_copy(refs[i].at[pl.ds(j * half, half)], refs[4 + i].at[pl.ds(j * half, half)], sem.at[i, j])
+        for i in range(4) for j in range(2)
+    ]
     for cp in copies:
         cp.start()
     for cp in copies:
@@ -365,7 +373,7 @@
         out_shape=(shape,) * 4,
         in_specs=[vmem] * 4,
         out_specs=(hbm,) * 4,
-        scratch_shapes=[dma((4,))],
+        scratch_shapes=[dma((4, 2))],
     )(*(pltpu.with_memory_space_constraint(a, pltpu.VMEM) for a in outs))
 
 

time: 41.7 us -> 41.8 us (level)
  no operation moved by 1% of the time
where the time goes in v6:
time: 41.8 us; the launch traced here: 41.6 us
  Pallas kernels  41 us (98%)
  between operations  0.64 us (2%)
    pallas_call x1, Pallas kernels, body(): pl.pallas_call(functools.partial(kernel, nz, nb), out_shape=(pltpu.VMEM((...  39.6 us
    pallas_call x1, Pallas kernels, body(): pl.pallas_call(write_out, out_shape=(shape,) * 4, in_specs=[vmem] * 4, ou...  1.38 us

profile of v6, /device:TPU:8, one launch (start us, length us, event | category | flops | bytes accessed | tf_op | source)
XLA Modules:
  0.0 41.6 jit_solution(18423838624673963826)
XLA Ops:
  0.6 39.6 %shard_map.75 = (bf16[512,512]{1,0:T(8,128)(2,1)S(1)}, bf16[512,512]{1,0:T(8,128)(2,1)S(1)}, bf16[512,512]{1,0:T(8,128)(2,1)S(1)}, bf16[512,512]{1,0:T(8,128)(2,1)S(1)}) custom-call(bf16[512,512]{1,0:T(8,128)(2,1)} %q_hbm.1, bf16[512,512]{1,0:T(8,128)(2,1)} %k_hbm.1, bf16[512,512]{1,0:T(8,128)(2,1)} %v_hbm.1, bf16[512,512]{1,0:T(8,128)(2,1)} %g_hbm.1), custom_call_target="tpu_custom_call" | custom-call | tf_op jit(solution)/shard_map/pallas_call | solution.py:341
  40.3 1.4 %shard_map.76 = (bf16[512,512]{1,0:T(8,128)(2,1)}, bf16[512,512]{1,0:T(8,128)(2,1)}, bf16[512,512]{1,0:T(8,128)(2,1)}, bf16[512,512]{1,0:T(8,128)(2,1)}) custom-call(bf16[512,512]{1,0:T(8,128)(2,1)S(1)} %get-tuple-element.8.refs_0_, bf16[512,512]{1,0:T(8,128)(2,1)S(1)} %get-tuple-element.9.refs_1_, bf16[512,512]{1,0:T(8,128)(2,1)S(1)} %get-tuple-element.10.refs_2_, ...), custom_call_target="tpu_custom_call" | custom-call | tf_op jit(solution)/shard_map/pallas_call | solution.py:371
